TPU v7x, 32 devices: a whole 2x2x4 slice. The times are simulated.
32 devices in a mesh: dp: 8 (over z, x), ctx: 4 (over y, core).
Axes of the slice: x: 2, y: 2, z: 4, core: 2. Of those that a mesh axis runs over, the one named last changes fastest.
Arguments:
- tokens: bfloat16 [64, 1024, 576], P('dp', 'ctx'), may hold values from -6 to 6
- w_qkv: bfloat16 [552960], P(('dp', 'ctx')), may hold values from -0.25 to 0.25
- w_out: bfloat16 [331776], P(('dp', 'ctx')), may hold values from -1 to 1
- w_gate_up: bfloat16 [1769472], P(('dp', 'ctx')), may hold values from -0.25 to 0.25
- w_down: bfloat16 [884736], P(('dp', 'ctx')), may hold values from -0.15625 to 0.15625
- gains: bfloat16 [1152], P(('dp', 'ctx')), may hold values from 0.099609375 to 1.8984375
- cotangent: bfloat16 [64, 1024, 576], P('dp', 'ctx'), may hold values from -6 to 6
Outputs:
- output: bfloat16 [64, 1024, 576], P('dp', 'ctx')
- grad_input: bfloat16 [64, 1024, 576], P('dp', 'ctx')
- grad_qkv: float32 [552960], P(('dp', 'ctx'))
- grad_out: float32 [331776], P(('dp', 'ctx'))
- grad_gate_up: float32 [1769472], P(('dp', 'ctx'))
- grad_down: float32 [884736], P(('dp', 'ctx'))
- grad_gains: float32 [1152], P(('dp', 'ctx'))
All inputs are finite; a program needn't handle non-finite values.
Results may differ from a plain program's by a relative error of at most 0.014.
Values may be sent and summed in bfloat16 or wider, within the bound.
No kernel may reach another device: no remote copies, remote signals or barrier semaphores. Data moves between devices by JAX's collectives and lax.ppermute only.
A program may use at most 384 MiB of HBM per device.

v0:
```python
import math
import jax
import jax.numpy as jnp
from jax import lax
from jax.sharding import PartitionSpec as P

D = 576
HEADS = 9
KV_HEADS = 3
HEAD = 64
FF = 1536
QKVW = 960
EPSILON = 1e-05
THETA_BASE = 100000.0
NEG_FILL = -1e30


def angle_tables(positions, width):
    halves = jnp.arange(0, width, 2).astype(jnp.float32) / width
    inverse = jnp.exp(-math.log(THETA_BASE) * halves)
    angles = positions.astype(jnp.float32)[:, None] * inverse[None, :]
    angles = jnp.concatenate([angles, angles], axis=-1)
    return (jnp.cos(angles), jnp.sin(angles))


def rotate(values, cosine, sine):
    half = values.shape[-1] // 2
    turned = jnp.concatenate([-values[..., half:], values[..., :half]], axis=-1)
    return values * cosine + turned * sine


def unrotate(grads, cosine, sine):
    half = grads.shape[-1] // 2
    scaled = grads * sine
    turned = jnp.concatenate([scaled[..., half:], -scaled[..., :half]], axis=-1)
    return grads * cosine + turned


def fetch(part_qkv, part_out, part_gu, part_down, part_gains):
    result = (
        lax.all_gather(part_qkv, ("dp", "ctx"), axis=0, tiled=True),
        lax.all_gather(part_out, ("dp", "ctx"), axis=0, tiled=True),
        lax.all_gather(part_gu, ("dp", "ctx"), axis=0, tiled=True),
        lax.all_gather(part_down, ("dp", "ctx"), axis=0, tiled=True),
        lax.all_gather(part_gains, ("dp", "ctx"), axis=0, tiled=True),
    )
    return result


def settle(term_qkv, term_out, term_gu, term_down, term_gains):
    result = (
        lax.psum_scatter(term_qkv, ("dp", "ctx"), scatter_dimension=0, tiled=True),
        lax.psum_scatter(term_out, ("dp", "ctx"), scatter_dimension=0, tiled=True),
        lax.psum_scatter(term_gu, ("dp", "ctx"), scatter_dimension=0, tiled=True),
        lax.psum_scatter(term_down, ("dp", "ctx"), scatter_dimension=0, tiled=True),
        lax.psum_scatter(term_gains, ("dp", "ctx"), scatter_dimension=0, tiled=True),
    )
    return result


def attention_scores(queries, keys, allowed):
    raw = jnp.einsum("sqhgd,skhd->shgqk", queries, keys, preferred_element_type=jnp.float32) * 0.125
    return jnp.where(allowed, raw, NEG_FILL)


def local(tokens, w_qkv, w_out, w_gate_up, w_down, gains, cotangent):
    seqs_here = tokens.shape[0]
    span = tokens.shape[1]
    group = HEADS // KV_HEADS
    kv_width = KV_HEADS * HEAD
    row_count = seqs_here * span
    first = fetch(w_qkv, w_out, w_gate_up, w_down, gains)
    mat_qkv = first[0].reshape(D, QKVW)
    mat_out = first[1].reshape(D, D)
    mat_gu = first[2].reshape(D, 2 * FF)
    mat_down = first[3].reshape(FF, D)
    gain_one = first[4][:D].astype(jnp.float32)
    gain_two = first[4][D:].astype(jnp.float32)
    rows = tokens.reshape(row_count, D).astype(jnp.float32)
    inverse_one = lax.rsqrt(jnp.mean(rows * rows, axis=-1, keepdims=True) + EPSILON)
    normal_one = rows * inverse_one
    normed_one = (normal_one * gain_one).astype(jnp.bfloat16)
    projected = jnp.dot(normed_one, mat_qkv, preferred_element_type=jnp.float32)
    here = lax.axis_index("ctx") * span + jnp.arange(span)
    cos_here, sin_here = angle_tables(here, HEAD)
    cos_q = cos_here[None, :, None, :]
    sin_q = sin_here[None, :, None, :]
    queries = rotate(projected[:, :D].reshape(seqs_here, span, HEADS, HEAD), cos_q, sin_q)
    query_low = queries.astype(jnp.bfloat16).reshape(seqs_here, span, KV_HEADS, group, HEAD)
    key_low = rotate(
        projected[:, D : D + kv_width].reshape(seqs_here, span, KV_HEADS, HEAD), cos_q, sin_q
    ).astype(jnp.bfloat16)
    value_low = projected[:, D + kv_width :].astype(jnp.bfloat16)
    stacked = jnp.concatenate(
        [key_low.reshape(seqs_here, span, kv_width), value_low.reshape(seqs_here, span, kv_width)],
        axis=-1,
    )
    gathered = lax.all_gather(stacked, "ctx", axis=1, tiled=True)
    total_len = gathered.shape[1]
    key_all = gathered[..., :kv_width].reshape(seqs_here, total_len, KV_HEADS, HEAD)
    value_all = gathered[..., kv_width:].reshape(seqs_here, total_len, KV_HEADS, HEAD)
    places = jnp.arange(total_len)
    allowed = here[:, None] >= places[None, :]
    scores = attention_scores(query_low, key_all, allowed)
    highest = jnp.max(scores, axis=-1, keepdims=True)
    expo = jnp.exp(scores - highest)
    totals = jnp.sum(expo, axis=-1, keepdims=True)
    probs = expo / totals
    log_total = highest + jnp.log(totals)
    prob_low = probs.astype(jnp.bfloat16)
    mixed = jnp.einsum("shgqk,skhd->sqhgd", prob_low, value_all, preferred_element_type=jnp.float32)
    mixed_low = mixed.reshape(row_count, D).astype(jnp.bfloat16)
    residual = rows + jnp.dot(mixed_low, mat_out, preferred_element_type=jnp.float32)
    inverse_two = lax.rsqrt(jnp.mean(residual * residual, axis=-1, keepdims=True) + EPSILON)
    normal_two = residual * inverse_two
    normed_two = (normal_two * gain_two).astype(jnp.bfloat16)
    gate_up = jnp.dot(normed_two, mat_gu, preferred_element_type=jnp.float32)
    gate_part = gate_up[:, :FF]
    up_part = gate_up[:, FF:]
    sigmoid_gate = 1.0 / (1.0 + jnp.exp(-gate_part))
    activated = gate_part * sigmoid_gate
    product_low = (activated * up_part).astype(jnp.bfloat16)
    output = (residual + jnp.dot(product_low, mat_down, preferred_element_type=jnp.float32)).astype(
        jnp.bfloat16
    )
    second = fetch(w_qkv, w_out, w_gate_up, w_down, gains)
    back_qkv = second[0].reshape(D, QKVW)
    back_out = second[1].reshape(D, D)
    back_gu = second[2].reshape(D, 2 * FF)
    back_down = second[3].reshape(FF, D)
    grad_rows = cotangent.reshape(row_count, D)
    grad_down = jnp.dot(product_low.T, grad_rows, preferred_element_type=jnp.float32)
    grad_product = jnp.dot(grad_rows, back_down.T, preferred_element_type=jnp.float32)
    grad_gate = grad_product * up_part * sigmoid_gate * (1.0 + gate_part * (1.0 - sigmoid_gate))
    grad_up = grad_product * activated
    grad_gu_low = jnp.concatenate([grad_gate, grad_up], axis=-1).astype(jnp.bfloat16)
    grad_gate_up = jnp.dot(normed_two.T, grad_gu_low, preferred_element_type=jnp.float32)
    grad_normed_two = jnp.dot(grad_gu_low, back_gu.T, preferred_element_type=jnp.float32)
    grad_gain_two = jnp.sum(grad_normed_two * normal_two, axis=0)
    scaled_two = grad_normed_two * gain_two
    grad_residual = grad_rows.astype(jnp.float32) + inverse_two * (
        scaled_two - normal_two * jnp.mean(scaled_two * normal_two, axis=-1, keepdims=True)
    )
    grad_branch_low = grad_residual.astype(jnp.bfloat16)
    grad_out = jnp.dot(mixed_low.T, grad_branch_low, preferred_element_type=jnp.float32)
    grad_mixed_low = jnp.dot(
        grad_branch_low, back_out.T, preferred_element_type=jnp.float32
    ).astype(jnp.bfloat16)
    grad_mixed_low = grad_mixed_low.reshape(seqs_here, span, KV_HEADS, group, HEAD)
    scores_again = attention_scores(query_low, key_all, allowed)
    probs_again = jnp.exp(scores_again - log_total)
    prob_again_low = probs_again.astype(jnp.bfloat16)
    grad_probs = jnp.einsum(
        "sqhgd,skhd->shgqk", grad_mixed_low, value_all, preferred_element_type=jnp.float32
    )
    centre = jnp.sum(probs_again * grad_probs, axis=-1, keepdims=True)
    grad_scores_low = (probs_again * (grad_probs - centre)).astype(jnp.bfloat16)
    grad_queries = 0.125 * jnp.einsum(
        "shgqk,skhd->sqhgd", grad_scores_low, key_all, preferred_element_type=jnp.float32
    )
    grad_keys = 0.125 * jnp.einsum(
        "shgqk,sqhgd->skhd", grad_scores_low, query_low, preferred_element_type=jnp.float32
    )
    grad_values = jnp.einsum(
        "shgqk,sqhgd->skhd", prob_again_low, grad_mixed_low, preferred_element_type=jnp.float32
    )
    cos_all, sin_all = angle_tables(places, HEAD)
    grad_queries = unrotate(grad_queries.reshape(seqs_here, span, HEADS, HEAD), cos_q, sin_q)
    grad_keys = unrotate(grad_keys, cos_all[None, :, None, :], sin_all[None, :, None, :])
    kv_terms = jnp.concatenate(
        [
            grad_keys.reshape(seqs_here, total_len, kv_width),
            grad_values.reshape(seqs_here, total_len, kv_width),
        ],
        axis=-1,
    ).astype(jnp.bfloat16)
    kv_owned = lax.psum_scatter(kv_terms, "ctx", scatter_dimension=1, tiled=True).astype(
        jnp.float32
    )
    grad_proj_low = jnp.concatenate(
        [grad_queries.reshape(row_count, D), kv_owned.reshape(row_count, 2 * kv_width)], axis=-1
    ).astype(jnp.bfloat16)
    grad_qkv = jnp.dot(normed_one.T, grad_proj_low, preferred_element_type=jnp.float32)
    grad_normed_one = jnp.dot(grad_proj_low, back_qkv.T, preferred_element_type=jnp.float32)
    grad_gain_one = jnp.sum(grad_normed_one * normal_one, axis=0)
    scaled_one = grad_normed_one * gain_one
    grad_input = grad_residual + inverse_one * (
        scaled_one - normal_one * jnp.mean(scaled_one * normal_one, axis=-1, keepdims=True)
    )
    owned = settle(
        grad_qkv.reshape(-1),
        grad_out.reshape(-1),
        grad_gate_up.reshape(-1),
        grad_down.reshape(-1),
        jnp.concatenate([grad_gain_one, grad_gain_two]),
    )
    return (
        output.reshape(tokens.shape),
        grad_input.astype(jnp.bfloat16).reshape(tokens.shape),
        owned[0],
        owned[1],
        owned[2],
        owned[3],
        owned[4],
    )


def solution(mesh):
    in_specs = (
        P("dp", "ctx", None),
        P(("dp", "ctx")),
        P(("dp", "ctx")),
        P(("dp", "ctx")),
        P(("dp", "ctx")),
        P(("dp", "ctx")),
        P("dp", "ctx", None),
    )
    out_specs = (
        P("dp", "ctx", None),
        P("dp", "ctx", None),
        P(("dp", "ctx")),
        P(("dp", "ctx")),
        P(("dp", "ctx")),
        P(("dp", "ctx")),
        P(("dp", "ctx")),
    )
    return jax.shard_map(local, mesh=mesh, in_specs=in_specs, out_specs=out_specs, check_vma=False)
```

profile of v0, /device:TPU:0, one launch (start us, length us, event | category | flops | bytes accessed | tf_op | source)
XLA Modules:
  0.0 946.1 jit_solution(13876361599420750853)
XLA Ops:
  11.1 42.0 %all-reduce = bf16[1152]{0:T(1024)(128)(2,1)S(1)} all-reduce(bf16[1152]{0:T(1024)(128)(2,1)S(1)} %dynamic-update-slice), channel_id=1, replica_groups=mesh['dp'=8,'ctx'=4] {'dp','ctx'}, use_global_device_ids=true, to_apply=%add | all-reduce | flops 1152 | bytes 4608
  59.9 11.1 %all-gather.13.cloned.1.call-done = bf16[32,1,17280]{2,1,0:T(2,128)(2,1)} async-done(((bf16[1,1,17280]{2,1,0:T(2,128)(2,1)}), bf16[32,1,17280]{2,1,0:T(2,128)(2,1)}) %all-gather.13.cloned.1.call-update) | async-done | bytes 1105936 | tf_op jit(solution)/shard_map/all_gather | solution.py:41
  71.0 7.7 reduce.1
  80.8 4.7 fusion.55
  90.7 46.2 %all-gather.1 = bf16[32,1,10368]{2,1,0:T(2,128)(2,1)} all-gather(bf16[1,1,10368]{2,1,0:T(2,128)(2,1)S(1)} %reshape.317), channel_id=1, replica_groups=mesh['dp'=8,'ctx'=4] {'dp','ctx'}, dimensions={0}, use_global_device_ids=true | all-gather | bytes 684288 | tf_op jit(solution)/shard_map/all_gather | solution.py:42
  136.9 5.0 reduce.2
  143.7 3.4 copy.96
  147.5 2.8 copy.94
  161.3 4.7 reshape.298
  165.9 25.6 %all-gather.9.cloned.1.call-done = bf16[1769472]{0:T(1024)(128)(2,1)} async-done(((bf16[55296]{0:T(1024)(128)(2,1)}), bf16[1769472]{0:T(1024)(128)(2,1)}) %all-gather.9.cloned.1.call-update) | async-done | bytes 3538960 | tf_op jit(solution)/shard_map/all_gather | solution.py:43
  191.5 6.9 reshape.297
  198.5 41.1 %all-gather.7.cloned.1.call-done = bf16[8,1024,384]{1,0,2:T(8,128)(2,1)} async-done(((bf16[8,256,384]{1,0,2:T(8,128)(2,1)}), bf16[8,1024,384]{1,0,2:T(8,128)(2,1)}) %all-gather.7.cloned.1.call-update) | async-done | bytes 6291472 | tf_op jit(solution)/shard_map/all_gather | solution.py:98
  239.6 3.6 fusion.53
  244.9 3.5 copy.59
  248.4 27.1 %fusion.9 = (f32[8,3,3,256]{3,2,1,0:T(4,128)S(1)}, f32[8,3,1024,256,3]{3,2,4,1,0:T(8,128)}) fusion(pred[256,1024]{0,1:T(8,128)(4,1)S(1)} %iota_compare_fusion, bf16[8,1024,3,64,1]{1,3,4,2,0:T(8,128)(2,1)S(1)} %bitcast.178, bf16[8,256,3,3,64]{1,4,3,2,0:T(8,128)(2,1)S(1)} %fusion.18), kind=kOutput, calls=%fused_computation.14 | convolution fusion | flops 2472523776 | bytes 81338368 | tf_op jit(solution)/shard_map/sqhgd,skhd->shgqk/dot_general | solution.py:62
  275.5 24.8 %fusion.3 = f32[8,3,3,256]{3,2,1,0:T(4,128)} fusion(f32[8,3,3,256]{3,2,1,0:T(4,128)S(1)} %get-tuple-element.57, f32[8,3,1024,256,3]{3,2,4,1,0:T(8,128)} %get-tuple-element.58, pred[256,1024]{0,1:T(8,128)(4,1)S(1)} %iota_compare_fusion), kind=kLoop, calls=%fused_computation.9 | loop fusion | flops 75479040 | bytes 75907072 | tf_op jit(solution)/shard_map/reduce_sum | solution.py:107
  301.9 29.8 %convert_bitcast_fusion.1 = bf16[8,256,3,3,64]{1,4,3,2,0:T(8,128)(2,1)} fusion(bf16[8,1024,3,64,1]{1,3,4,2,0:T(8,128)(2,1)S(1)} %bitcast.194, f32[8,3,3,256]{3,2,1,0:T(4,128)} %fusion.3, f32[8,3,3,256]{3,2,1,0:T(4,128)S(1)} %get-tuple-element.57, f32[8,3,1024,256,3]{3,2,4,1,0:T(8,128)} %get-tuple-element.58, pred[256,1024]{0,1:T(8,128)(4,1)S(1)} %iota_compare_fusion), kind=kOutput, calls=%fused_computation.67 | convolution fusion | flops 2511470592 | bytes 81412096 | tf_op jit(solution)/shard_map/shgqk,skhd->sqhgd/dot_general | solution.py:111
  331.8 3.2 copy.65
  335.8 5.5 multiply_reduce_fusion.4
  341.3 14.0 %fusion.51 = f32[2048,3072]{1,0:T(8,128)} fusion(bf16[576,3072]{1,0:T(8,128)(2,1)S(1)} %copy-done.15, f32[2048,576]{0,1:T(8,128)S(1)} %get-tuple-element.60, f32[576]{0:T(1024)S(1)} %copy-done.34, f32[2048]{0:T(1024)S(1)} %add_rsqrt_fusion), kind=kOutput, calls=%fused_computation.114 | convolution fusion | flops 7251296256 | bytes 33433856 | tf_op jit(solution)/shard_map/dot_general | solution.py:117
  355.3 21.5 %multiply_convert_fusion.1 = (bf16[2048,1536]{1,0:T(8,128)(2,1)}, bf16[2048,1536]{1,0:T(8,128)(2,1)}, bf16[2048,1536]{1,0:T(8,128)(2,1)}) fusion(f32[2048,3072]{1,0:T(8,128)} %fusion.51, bf16[2048,576]{0,1:T(8,128)(2,1)} %bitcast.197, bf16[1536,576]{1,0:T(8,128)(2,1)} %reshape.298), kind=kOutput, calls=%fused_computation.17 | convolution fusion | flops 3671064576 | bytes 48168960 | tf_op jit(solution)/shard_map/dot_general | solution.py:133
  376.8 13.5 %multiply_reduce_fusion = (f32[576]{0:T(1024)}, f32[2048]{0:T(1024)S(1)}, f32[2048,576]{0,1:T(8,128)S(1)}) fusion(f32[2048,576]{0,1:T(8,128)} %copy-done, f32[2048]{0:T(1024)S(1)} %add_rsqrt_fusion, f32[576]{0:T(1024)S(1)} %copy-done.34, bf16[576,3072]{1,0:T(8,128)(2,1)} %reshape.297, bf16[2048,1536]{1,0:T(8,128)(2,1)} %get-tuple-element.37, ...), kind=kOutput, calls=%fused_computation.41 | convolution fusion | flops 7279998464 | bytes 25580032 | tf_op jit(solution)/shard_map/dot_general | solution.py:138
  396.3 30.7 %bitcast_convert_fusion = bf16[8,3,64,1024]{3,2,1,0:T(8,128)(2,1)} fusion(f32[8,3,3,256]{3,2,1,0:T(4,128)S(1)} %copy-done.26, f32[8,3,1024,256,3]{3,2,4,1,0:T(8,128)} %get-tuple-element.58, pred[256,1024]{0,1:T(8,128)(4,1)S(1)} %iota_compare_fusion, bf16[8,256,3,3,64]{1,0,4,3,2:T(8,128)(2,1)S(1)} %bitcast.203), kind=kOutput, calls=%fused_computation.29 | convolution fusion | flops 2492989440 | bytes 81338368 | tf_op jit(solution)/shard_map/shgqk,sqhgd->skhd/dot_general | solution.py:164
  427.0 57.9 %fusion = (f32[8,3,3,256]{3,2,1,0:T(4,128)}, f32[8,3,1024,256,3]{3,2,4,1,0:T(8,128)}) fusion(f32[8,3,3,256]{3,2,1,0:T(4,128)S(1)} %copy-done.26, f32[8,3,1024,256,3]{3,2,4,1,0:T(8,128)} %get-tuple-element.58, pred[256,1024]{0,1:T(8,128)(4,1)S(1)} %iota_compare_fusion, bf16[8,1024,3,64,1]{1,3,4,2,0:T(8,128)(2,1)S(1)} %bitcast.195, ...), kind=kOutput, calls=%fused_computation.2 | convolution fusion | flops 2510272512 | bytes 156909568 | tf_op jit(solution)/shard_map/sqhgd,skhd->shgqk/dot_general | solution.py:153
  484.9 6.2 copy.77
  491.1 59.9 %fusion.2 = bf16[8,3,3,256,1024]{3,4,2,1,0:T(8,128)(2,1)} fusion(f32[8,3,1024,256,3]{3,2,4,1,0:T(8,128)} %get-tuple-element.63, f32[8,3,3,256]{3,2,1,0:T(4,128)S(1)} %copy-done.27, f32[8,3,3,256]{3,2,1,0:T(4,128)S(1)} %copy-done.26, f32[8,3,1024,256,3]{3,2,4,1,0:T(8,128)} %get-tuple-element.58, pred[256,1024]{0,1:T(8,128)(4,1)S(1)} %iota_compare_fusion), kind=kLoop, calls=%fused_computation.4 | loop fusion | flops 113246208 | bytes 189153280 | tf_op jit(solution)/shard_map/convert_element_type | solution.py:157
  551.0 19.4 %bitcast_multiply_fusion.1 = (f32[8,1024,3,64]{1,3,2,0:T(8,128)S(1)}, f32[8,3,64,1024,1]{3,2,4,1,0:T(8,128)}) fusion(f32[1024,64]{0,1:T(8,128)S(1)} %copy-done.6, bf16[8,256,3,3,64]{1,4,3,2,0:T(8,128)(2,1)} %copy-done.5, bf16[8,3,3,256,1024]{3,4,2,1,0:T(8,128)(2,1)} %fusion.2), kind=kOutput, calls=%fused_computation.30 | convolution fusion | flops 2417491968 | bytes 52953088 | tf_op jit(solution)/shard_map/shgqk,sqhgd->skhd/dot_general | solution.py:161
  572.9 5.5 fusion.13
  578.3 4.1 copy.76
  582.5 8.4 pad_maximum_fusion.3
  592.2 4.4 copy.106
  596.6 8.9 fusion.56
  605.5 5.3 reshape.311
  610.8 13.1 %fusion.19 = f32[72,24,8,128]{3,2,1,0:T(8,128)S(1)} fusion(bf16[2048,1536]{1,0:T(8,128)(2,1)} %get-tuple-element.37, bf16[2048,1536]{1,0:T(8,128)(2,1)} %get-tuple-element.36, f32[2048,576]{0,1:T(8,128)} %copy-done, f32[576]{0:T(1024)S(1)} %copy-done.35, f32[2048]{0:T(1024)S(1)} %copy-done.31), kind=kOutput, calls=%fused_computation.56 | convolution fusion | flops 7276462080 | bytes 24389888 | tf_op jit(solution)/shard_map/dot_general | solution.py:137
  623.8 4.5 copy.108
  628.3 5.7 fusion.32
  634.0 2.8 reshape.309
  636.8 18.1 %broadcast_multiply_fusion = f32[8,3,64,3,256]{4,2,3,1,0:T(8,128)} fusion(bf16[8,1024,3,64,1]{1,3,4,2,0:T(8,128)(2,1)S(1)} %bitcast.179, bf16[8,3,3,256,1024]{3,4,2,1,0:T(8,128)(2,1)} %fusion.2), kind=kOutput, calls=%fused_computation.65 | convolution fusion | flops 2417098752 | bytes 45613056 | tf_op jit(solution)/shard_map/shgqk,skhd->sqhgd/dot_general | solution.py:158
  654.9 5.2 copy_multiply_fusion
  663.1 2.7 copy.71
  668.1 2.7 add_convert_fusion.1
  670.8 2.8 copy.78
  673.6 6.2 fusion.22
  683.7 8.2 add_convert_fusion.2
  695.0 4.5 multiply_reduce_fusion.1
  699.5 4.3 add_convert_fusion
  705.4 41.2 %all-reduce.5 = f32[1152]{0:T(1024)S(1)} all-reduce(f32[1152]{0:T(1024)S(1)} %pad_maximum_fusion.14), channel_id=7, replica_groups=mesh['dp'=8,'ctx'=4] {'dp','ctx'}, use_global_device_ids=true, to_apply=%region_14.15.clone | all-reduce | flops 1152 | bytes 9216
  747.2 185.5 %all-reduce.9.cloned.1.call-done = (f32[552960]{0:T(1024)}, f32[331776]{0:T(1024)}, f32[1769472]{0:T(1024)}, f32[884736]{0:T(1024)}) async-done(((f32[552960]{0:T(1024)}, f32[331776]{0:T(1024)}, f32[1769472]{0:T(1024)}, f32[884736]{0:T(1024)}), (f32[552960]{0:T(1024)}, f32[331776]{0:T(1024)}, f32[1769472]{0:T(1024)}, f32[884736]{0:T(1024)})) %all-reduce.9.cloned.1.call-update) | async-done | bytes 14155792
  (165 shorter events, 65.2 us)
Async XLA Ops:
  7.2 63.9 %all-gather.13.cloned.1.call-start = ((), (), s32[]{:S(2)}) async-start(), calls=%async_computation.5 | async-start | bytes 2280960 | tf_op jit(solution)/shard_map/all_gather | solution.py:41
  8.7 152.6 %all-gather.11.cloned.1.call-start = ((), (), s32[]{:S(2)}) async-start(), calls=%async_computation.3 | async-start | bytes 1824768 | tf_op jit(solution)/shard_map/all_gather | solution.py:44
  9.4 182.1 %all-gather.9.cloned.1.call-start = ((), (), s32[]{:S(2)}) async-start(), calls=%async_computation.2 | async-start | bytes 3649536 | tf_op jit(solution)/shard_map/all_gather | solution.py:43
  10.2 229.4 %all-gather.7.cloned.1.call-start = ((), (), s32[]{:S(2)}) async-start(), calls=%async_computation.1 | async-start | bytes 7864320 | tf_op jit(solution)/shard_map/all_gather | solution.py:98
  53.8 2.8 copy-start.28
  59.9 99.2 %copy-start.22 = (f32[256,64]{0,1:T(8,128)}, f32[256,64]{0,1:T(8,128)S(1)}, u32[]{:S(2)}) copy-start(f32[256,64]{0,1:T(8,128)S(1)} %get-tuple-element.52) | copy-start | bytes 196612
  85.5 3.1 copy-start.7
  86.0 2.9 copy-start.24
  88.9 1.8 copy-start.33
  90.6 580.1 %reduce-scatter.2.cloned.1.call-start = ((), (), s32[]{:S(2)}) async-start(), calls=%async_computation.4 | async-start | bytes 7864320 | tf_op jit(solution)/shard_map/reduce_scatter | solution.py:177
  90.7 56.4 %copy-start.4 = (bf16[8,256,576]{1,2,0:T(8,128)(2,1)S(1)}, bf16[8,256,576]{1,2,0:T(8,128)(2,1)}, u32[]{:S(2)}) copy-start(bf16[8,256,576]{1,2,0:T(8,128)(2,1)} %param.7) | copy-start | bytes 7077892
  152.6 2.3 slice-start.4
  161.2 87.1 %copy-start.5 = (bf16[8,256,3,3,64]{1,4,3,2,0:T(8,128)(2,1)}, bf16[8,256,3,3,64]{1,4,3,2,0:T(8,128)(2,1)S(1)}, u32[]{:S(2)}) copy-start(bf16[8,256,3,3,64]{1,4,3,2,0:T(8,128)(2,1)S(1)} %fusion.18) | copy-start | bytes 7077892
  244.8 30.7 %copy-start.2 = (bf16[8,1024,192]{1,2,0:T(8,128)(2,1)}, bf16[8,1024,192]{1,2,0:T(8,128)(2,1)S(1)}, u32[]{:S(2)}) copy-start(bf16[8,1024,192]{1,2,0:T(8,128)(2,1)S(1)} %copy.60) | copy-start | bytes 9437188
  275.5 26.4 %copy-start.11 = (bf16[8,1024,192]{1,2,0:T(8,128)(2,1)S(1)}, bf16[8,1024,192]{1,2,0:T(8,128)(2,1)}, u32[]{:S(2)}) copy-start(bf16[8,1024,192]{1,2,0:T(8,128)(2,1)} %copy.59) | copy-start | bytes 9437188
  331.8 4.0 copy-start.16
  335.7 5.5 copy-start.9
  335.8 5.6 copy-start.15
  335.8 5.6 copy-start.34
  341.3 14.0 %copy-start = (f32[2048,576]{0,1:T(8,128)}, f32[2048,576]{0,1:T(8,128)S(1)}, u32[]{:S(2)}) copy-start(f32[2048,576]{0,1:T(8,128)S(1)} %get-tuple-element.60) | copy-start | bytes 14155780
  341.3 49.0 %copy-start.30 = (f32[2048]{0:T(1024)}, f32[2048]{0:T(1024)S(1)}, u32[]{:S(2)}) copy-start(f32[2048]{0:T(1024)S(1)} %add_rsqrt_fusion) | copy-start | bytes 24580
  376.8 13.5 %copy-start.1 = (f32[2048,576]{0,1:T(8,128)S(1)}, f32[2048,576]{0,1:T(8,128)}, u32[]{:S(2)}) copy-start(f32[2048,576]{0,1:T(8,128)} %copy-done) | copy-start | bytes 14155780
  376.8 13.5 %copy-start.12 = (bf16[8,72,8,256]{3,2,0,1:T(8,128)(2,1)S(1)}, bf16[8,72,8,256]{3,2,0,1:T(8,128)(2,1)}, u32[]{:S(2)}) copy-start(bf16[8,72,8,256]{3,2,0,1:T(8,128)(2,1)} %copy.96) | copy-start | bytes 7077892
  390.3 1.6 copy-start.17
  391.9 2.2 copy-start.8
  394.1 2.2 copy-start.26
  394.9 1.4 copy-start.14
  484.9 6.2 copy-start.27
  491.1 59.9 %copy-start.6 = (f32[1024,64]{0,1:T(8,128)S(1)}, f32[1024,64]{0,1:T(8,128)}, u32[]{:S(2)}) copy-start(f32[1024,64]{0,1:T(8,128)} %get-tuple-element.50) | copy-start | bytes 786436
  570.5 2.4 copy-start.21
  590.9 341.8 %all-reduce.9.cloned.1.call-start = ((), (), s32[]{:S(2)}) async-start(), calls=%async_computation.6 | async-start | bytes 28311552
  592.2 4.4 copy-start.13
  605.5 5.3 copy-start.31
  605.5 5.3 copy-start.35
  623.8 4.5 copy-start.10
  628.3 8.5 copy-start.3
  636.8 18.1 %copy-start.23 = (f32[256,64]{0,1:T(8,128)S(1)}, f32[256,64]{0,1:T(8,128)}, u32[]{:S(2)}) copy-start(f32[256,64]{0,1:T(8,128)} %copy-done.22) | copy-start | bytes 196612
  660.4 2.6 slice-start.2
  660.7 2.3 slice-start.3
  663.1 5.0 slice-start.5
  665.8 2.3 slice-start.6
  668.1 5.4 copy-start.29
  682.2 1.5 copy-start.19
  682.2 11.3 %slice-start = ((s8[4718592]{0:T(1024)(128)(4,1)}), s8[524288]{0:T(1024)(128)(4,1)S(1)}, s32[]{:S(2)}) async-start(s8[4718592]{0:T(1024)(128)(4,1)} %bitcast.168), calls=%async_computation.7 | async-start | bytes 1048576
  683.7 9.8 %slice-start.1 = ((s8[4718592]{0:T(1024)(128)(4,1)}), s8[4194304]{0:T(1024)(128)(4,1)S(1)}, s32[]{:S(2)}) async-start(s8[4718592]{0:T(1024)(128)(4,1)} %bitcast.168), calls=%async_computation.8 | async-start | bytes 8388608
  691.9 2.6 copy-start.18
  691.9 3.0 copy-start.20
  703.8 1.6 copy-start.36
  (2 other events, 1.6 us)
Sparse Core Ops, SparseCore 0:
  11.4 59.5 all-gather.12
  73.8 56.0 all-gather.10
  132.9 58.5 all-gather.8
  193.5 46.0 all-gather.6
  591.0 58.3 reduce-scatter.1
  682.3 250.3 all-reduce.8
where the time goes:
time: 955 us; the launch traced here: 946 us
  matrix products  291 us (30%)
  waiting for transfers between devices  265 us (28%)
  other arithmetic  143 us (15%)
  blocking collectives  129 us (14%)
  local copies, waits for them, and re-layouts  102 us (11%)
  between operations  15.1 us (2%)
    unnamed x7, waiting for transfers between devices  187 us
    unnamed x2, blocking collectives  83.3 us
    convert_element_type x1, other arithmetic, local(): grad_scores_low = (probs_again * (grad_probs - centre)).astype(jnp.bfloat16)  59.9 us
    dot_general x1, matrix products, local(): jnp.einsum('sqhgd,skhd->shgqk', grad_mixed_low, value_all, preferred_elem...  57.9 us
    all_gather x1, blocking collectives, fetch(): lax.all_gather(part_out, ('dp', 'ctx'), axis=0, tiled=True)  46.2 us
    all_gather x1, waiting for transfers between devices, local(): gathered = lax.all_gather(stacked, 'ctx', axis=1, tiled=True)  41.1 us
    unnamed x105, local copies, waits for them, and re-layouts  34.6 us
    dot_general x1, matrix products, local(): jnp.einsum('shgqk,sqhgd->skhd', prob_again_low, grad_mixed_low, preferred...  30.7 us
  transfers between devices with their start and end apart: 6, of which 4 were waited for; matrix products, arithmetic and copies ran while one was open for 17% of the time, Pallas kernels for 0%

commit v1 on v0

--- a/solution.py
+++ b/solution.py
@@ -95,7 +95,12 @@
         [key_low.reshape(seqs_here, span, kv_width), value_low.reshape(seqs_here, span, kv_width)],
         axis=-1,
     )
-    gathered = lax.all_gather(stacked, "ctx", axis=1, tiled=True)
+    ring = [stacked]
+    for hop in range(3):
+        ring.append(lax.ppermute(ring[-1], "ctx", [(dev, (dev + 1) % 4) for dev in range(4)]))
+    gathered = jnp.roll(
+        jnp.concatenate(ring[::-1], axis=1), (lax.axis_index("ctx") + 1) * ring[0].shape[1], axis=1
+    )
     total_len = gathered.shape[1]
     key_all = gathered[..., :kv_width].reshape(seqs_here, total_len, KV_HEADS, HEAD)
     value_all = gathered[..., kv_width:].reshape(seqs_here, total_len, KV_HEADS, HEAD)

time: 955 us -> 940 us (0.984)
  waiting for transfers between devices: 265 us -> 237 us
    all_gather x1 -> x0, waiting for transfers between devices: 41.1 us -> none  [local(): gathered = lax.all_gather(stacked, 'ctx', axis=1, tiled=True)]
    ppermute x0 -> x3, waiting for transfers between devices: none -> 40.8 us  [local(): lax.ppermute(ring[-1], 'ctx', [(dev, (dev + 1) % 4) for dev in range(4)])]
    all_gather x1, waiting for transfers between devices: 25.6 us -> 0.01 us  [fetch(): lax.all_gather(part_gu, ('dp', 'ctx'), axis=0, tiled=True)]
    unnamed x105 -> x123, local copies, waits for them, and re-layouts: 34.6 us -> 42.3 us
    unnamed x7 -> x6, waiting for transfers between devices: 187 us -> 186 us
  transfers between devices with their start and end apart: 6 -> 8, of which waited for: 4 -> 4; matrix products, arithmetic and copies ran while one was open for 17% -> 17% of each run, Pallas kernels for 0% -> 0%
where the time goes in v1:
time: 940 us; the launch traced here: 931 us
  matrix products  291 us (31%)
  waiting for transfers between devices  237 us (25%)
  other arithmetic  144 us (15%)
  blocking collectives  135 us (14%)
  local copies, waits for them, and re-layouts  108 us (11%)
  between operations  14.9 us (2%)
    unnamed x6, waiting for transfers between devices  186 us
    unnamed x2, blocking collectives  80.2 us
    convert_element_type x1, other arithmetic, local(): grad_scores_low = (probs_again * (grad_probs - centre)).astype(jnp.bfloat16)  59.9 us
    dot_general x1, matrix products, local(): jnp.einsum('sqhgd,skhd->shgqk', grad_mixed_low, value_all, preferred_elem...  57.8 us
    all_gather x1, blocking collectives, fetch(): lax.all_gather(part_out, ('dp', 'ctx'), axis=0, tiled=True)  55.2 us
    unnamed x123, local copies, waits for them, and re-layouts  42.3 us
    ppermute x3, waiting for transfers between devices, local(): lax.ppermute(ring[-1], 'ctx', [(dev, (dev + 1) % 4) for dev in range(4)])  40.8 us
    dot_general x1, matrix products, local(): jnp.einsum('shgqk,sqhgd->skhd', prob_again_low, grad_mixed_low, preferred...  30.7 us
  transfers between devices with their start and end apart: 8, of which 4 were waited for; matrix products, arithmetic and copies ran while one was open for 17% of the time, Pallas kernels for 0%

profile of v1, /device:TPU:0, one launch (start us, length us, event | category | flops | bytes accessed | tf_op | source)
XLA Modules:
  0.0 931.0 jit_solution(6514824922681440657)
XLA Ops:
  11.1 42.0 %all-reduce = bf16[1152]{0:T(1024)(128)(2,1)S(1)} all-reduce(bf16[1152]{0:T(1024)(128)(2,1)S(1)} %dynamic-update-slice), channel_id=1, replica_groups=mesh['dp'=8,'ctx'=4] {'dp','ctx'}, use_global_device_ids=true, to_apply=%add | all-reduce | flops 1152 | bytes 4608
  59.9 11.1 %all-gather.10.cloned.1.call-done = bf16[32,1,17280]{2,1,0:T(2,128)(2,1)} async-done(((bf16[1,1,17280]{2,1,0:T(2,128)(2,1)}), bf16[32,1,17280]{2,1,0:T(2,128)(2,1)}) %all-gather.10.cloned.1.call-update) | async-done | bytes 1105936 | tf_op jit(solution)/shard_map/all_gather | solution.py:41
  71.0 7.7 reduce.1
  80.9 4.7 fusion.54
  89.8 20.4 %collective-permute-done = bf16[8,256,384]{1,0,2:T(8,128)(2,1)S(1)} collective-permute-done((bf16[8,256,384]{1,0,2:T(8,128)(2,1)S(1)}, bf16[8,256,384]{1,0,2:T(8,128)(2,1)S(1)}, u32[]{:S(2)}, u32[]{:S(2)}) %collective-permute-start) | collective-permute-done | bytes 1572896 | tf_op jit(solution)/shard_map/ppermute | solution.py:100
  110.2 2.7 convert_bitcast_fusion
  112.9 20.4 %collective-permute-done.1 = bf16[8,256,384]{1,0,2:T(8,128)(2,1)} collective-permute-done((bf16[8,256,384]{1,0,2:T(8,128)(2,1)S(1)}, bf16[8,256,384]{1,0,2:T(8,128)(2,1)}, u32[]{:S(2)}, u32[]{:S(2)}) %collective-permute-start.1) | collective-permute-done | bytes 1572896 | tf_op jit(solution)/shard_map/ppermute | solution.py:100
  133.3 55.2 %all-gather.1 = bf16[32,1,10368]{2,1,0:T(2,128)(2,1)S(1)} all-gather(bf16[1,1,10368]{2,1,0:T(2,128)(2,1)S(1)} %reshape.317), channel_id=1, replica_groups=mesh['dp'=8,'ctx'=4] {'dp','ctx'}, dimensions={0}, use_global_device_ids=true | all-gather | bytes 684288 | tf_op jit(solution)/shard_map/all_gather | solution.py:42
  188.5 4.0 reduce.2
  194.3 3.5 copy.96
  197.8 2.9 copy.94
  211.5 4.7 reshape.298
  216.2 6.9 reshape.297
  233.4 3.5 copy.59
  237.0 27.1 %fusion.9 = (f32[8,3,3,256]{3,2,1,0:T(4,128)S(1)}, f32[8,3,1024,256,3]{3,2,4,1,0:T(8,128)}) fusion(pred[256,1024]{0,1:T(8,128)(4,1)S(1)} %iota_compare_fusion, bf16[8,1024,3,64,1]{1,3,4,2,0:T(8,128)(2,1)S(1)} %bitcast.178, bf16[8,256,3,3,64]{1,4,3,2,0:T(8,128)(2,1)S(1)} %fusion.18), kind=kOutput, calls=%fused_computation.14 | convolution fusion | flops 2472523776 | bytes 81338368 | tf_op jit(solution)/shard_map/sqhgd,skhd->shgqk/dot_general | solution.py:62
  264.1 24.8 %fusion.3 = f32[8,3,3,256]{3,2,1,0:T(4,128)} fusion(f32[8,3,3,256]{3,2,1,0:T(4,128)S(1)} %get-tuple-element.57, f32[8,3,1024,256,3]{3,2,4,1,0:T(8,128)} %get-tuple-element.58, pred[256,1024]{0,1:T(8,128)(4,1)S(1)} %iota_compare_fusion), kind=kLoop, calls=%fused_computation.9 | loop fusion | flops 75479040 | bytes 75907072 | tf_op jit(solution)/shard_map/reduce_sum | solution.py:112
  290.5 29.8 %convert_bitcast_fusion.1 = bf16[8,256,3,3,64]{1,4,3,2,0:T(8,128)(2,1)} fusion(bf16[8,1024,3,64,1]{1,3,4,2,0:T(8,128)(2,1)S(1)} %bitcast.197, f32[8,3,3,256]{3,2,1,0:T(4,128)} %fusion.3, f32[8,3,3,256]{3,2,1,0:T(4,128)S(1)} %get-tuple-element.57, f32[8,3,1024,256,3]{3,2,4,1,0:T(8,128)} %get-tuple-element.58, pred[256,1024]{0,1:T(8,128)(4,1)S(1)} %iota_compare_fusion), kind=kOutput, calls=%fused_computation.67 | convolution fusion | flops 2511470592 | bytes 81412096 | tf_op jit(solution)/shard_map/shgqk,skhd->sqhgd/dot_general | solution.py:116
  320.3 3.2 copy.65
  324.4 5.5 multiply_reduce_fusion.4
  329.9 14.0 %fusion.51 = f32[2048,3072]{1,0:T(8,128)} fusion(bf16[576,3072]{1,0:T(8,128)(2,1)S(1)} %copy-done.20, f32[2048,576]{0,1:T(8,128)S(1)} %get-tuple-element.60, f32[576]{0:T(1024)S(1)} %copy-done.40, f32[2048]{0:T(1024)S(1)} %add_rsqrt_fusion), kind=kOutput, calls=%fused_computation.124 | convolution fusion | flops 7251296256 | bytes 33433856 | tf_op jit(solution)/shard_map/dot_general | solution.py:122
  343.9 21.5 %multiply_convert_fusion.1 = (bf16[2048,1536]{1,0:T(8,128)(2,1)}, bf16[2048,1536]{1,0:T(8,128)(2,1)}, bf16[2048,1536]{1,0:T(8,128)(2,1)}) fusion(f32[2048,3072]{1,0:T(8,128)} %fusion.51, bf16[2048,576]{0,1:T(8,128)(2,1)} %bitcast.200, bf16[1536,576]{1,0:T(8,128)(2,1)} %reshape.298), kind=kOutput, calls=%fused_computation.17 | convolution fusion | flops 3671064576 | bytes 48168960 | tf_op jit(solution)/shard_map/dot_general | solution.py:138
  365.4 13.5 %multiply_reduce_fusion = (f32[576]{0:T(1024)}, f32[2048]{0:T(1024)S(1)}, f32[2048,576]{0,1:T(8,128)S(1)}) fusion(f32[2048,576]{0,1:T(8,128)} %copy-done, f32[2048]{0:T(1024)S(1)} %add_rsqrt_fusion, f32[576]{0:T(1024)S(1)} %copy-done.40, bf16[576,3072]{1,0:T(8,128)(2,1)} %reshape.297, bf16[2048,1536]{1,0:T(8,128)(2,1)} %get-tuple-element.37, ...), kind=kOutput, calls=%fused_computation.41 | convolution fusion | flops 7279998464 | bytes 25580032 | tf_op jit(solution)/shard_map/dot_general | solution.py:143
  384.9 30.7 %bitcast_convert_fusion = bf16[8,3,64,1024]{3,2,1,0:T(8,128)(2,1)} fusion(f32[8,3,3,256]{3,2,1,0:T(4,128)S(1)} %copy-done.32, f32[8,3,1024,256,3]{3,2,4,1,0:T(8,128)} %get-tuple-element.58, pred[256,1024]{0,1:T(8,128)(4,1)S(1)} %iota_compare_fusion, bf16[8,256,3,3,64]{1,0,4,3,2:T(8,128)(2,1)S(1)} %bitcast.206), kind=kOutput, calls=%fused_computation.29 | convolution fusion | flops 2492989440 | bytes 81338368 | tf_op jit(solution)/shard_map/shgqk,sqhgd->skhd/dot_general | solution.py:169
  415.6 57.8 %fusion = (f32[8,3,3,256]{3,2,1,0:T(4,128)}, f32[8,3,1024,256,3]{3,2,4,1,0:T(8,128)}) fusion(f32[8,3,3,256]{3,2,1,0:T(4,128)S(1)} %copy-done.32, f32[8,3,1024,256,3]{3,2,4,1,0:T(8,128)} %get-tuple-element.58, pred[256,1024]{0,1:T(8,128)(4,1)S(1)} %iota_compare_fusion, bf16[8,1024,3,64,1]{1,3,4,2,0:T(8,128)(2,1)S(1)} %bitcast.198, ...), kind=kOutput, calls=%fused_computation.2 | convolution fusion | flops 2510272512 | bytes 156909568 | tf_op jit(solution)/shard_map/sqhgd,skhd->shgqk/dot_general | solution.py:158
  473.5 6.2 copy.77
  479.7 59.9 %fusion.2 = bf16[8,3,3,256,1024]{3,4,2,1,0:T(8,128)(2,1)} fusion(f32[8,3,1024,256,3]{3,2,4,1,0:T(8,128)} %get-tuple-element.63, f32[8,3,3,256]{3,2,1,0:T(4,128)S(1)} %copy-done.33, f32[8,3,3,256]{3,2,1,0:T(4,128)S(1)} %copy-done.32, f32[8,3,1024,256,3]{3,2,4,1,0:T(8,128)} %get-tuple-element.58, pred[256,1024]{0,1:T(8,128)(4,1)S(1)} %iota_compare_fusion), kind=kLoop, calls=%fused_computation.4 | loop fusion | flops 113246208 | bytes 189153280 | tf_op jit(solution)/shard_map/convert_element_type | solution.py:162
  539.6 19.4 %bitcast_multiply_fusion.1 = (f32[8,1024,3,64]{1,3,2,0:T(8,128)S(1)}, f32[8,3,64,1024,1]{3,2,4,1,0:T(8,128)}) fusion(f32[1024,64]{0,1:T(8,128)S(1)} %copy-done.6, bf16[8,256,3,3,64]{1,4,3,2,0:T(8,128)(2,1)} %copy-done.5, bf16[8,3,3,256,1024]{3,4,2,1,0:T(8,128)(2,1)} %fusion.2), kind=kOutput, calls=%fused_computation.30 | convolution fusion | flops 2417491968 | bytes 52953088 | tf_op jit(solution)/shard_map/shgqk,sqhgd->skhd/dot_general | solution.py:166
  561.5 5.5 fusion.13
  567.0 4.1 copy.76
  571.1 8.4 pad_maximum_fusion.3
  580.8 5.1 copy.106
  585.9 9.0 fusion.55
  594.9 5.4 reshape.311
  600.3 12.0 %fusion.19 = f32[72,24,8,128]{3,2,1,0:T(8,128)S(1)} fusion(bf16[2048,1536]{1,0:T(8,128)(2,1)} %get-tuple-element.37, bf16[2048,1536]{1,0:T(8,128)(2,1)} %get-tuple-element.36, f32[2048,576]{0,1:T(8,128)} %copy-done, f32[576]{0:T(1024)S(1)} %copy-done.41, f32[2048]{0:T(1024)S(1)} %copy-done.37), kind=kOutput, calls=%fused_computation.56 | convolution fusion | flops 7276462080 | bytes 24389888 | tf_op jit(solution)/shard_map/dot_general | solution.py:142
  612.4 4.4 copy.108
  616.8 5.7 fusion.32
  622.5 2.8 reshape.309
  625.4 18.2 %broadcast_multiply_fusion = f32[8,3,64,3,256]{4,2,3,1,0:T(8,128)} fusion(bf16[8,1024,3,64,1]{1,3,4,2,0:T(8,128)(2,1)S(1)} %bitcast.179, bf16[8,3,3,256,1024]{3,4,2,1,0:T(8,128)(2,1)} %fusion.2), kind=kOutput, calls=%fused_computation.65 | convolution fusion | flops 2417098752 | bytes 45613056 | tf_op jit(solution)/shard_map/shgqk,skhd->sqhgd/dot_general | solution.py:163
  643.6 5.2 copy_multiply_fusion
  651.7 2.7 copy.71
  656.8 2.7 add_convert_fusion.1
  659.4 2.8 copy.78
  662.2 6.2 fusion.22
  672.4 9.2 add_convert_fusion.2
  684.6 4.4 multiply_reduce_fusion.1
  689.0 4.4 add_convert_fusion
  695.0 38.2 %all-reduce.5 = f32[1152]{0:T(1024)S(1)} all-reduce(f32[1152]{0:T(1024)S(1)} %pad_maximum_fusion.14), channel_id=7, replica_groups=mesh['dp'=8,'ctx'=4] {'dp','ctx'}, use_global_device_ids=true, to_apply=%region_14.15.clone | all-reduce | flops 1152 | bytes 9216
  733.8 184.1 %all-reduce.9.cloned.1.call-done = (f32[552960]{0:T(1024)}, f32[331776]{0:T(1024)}, f32[1769472]{0:T(1024)}, f32[884736]{0:T(1024)}) async-done(((f32[552960]{0:T(1024)}, f32[331776]{0:T(1024)}, f32[1769472]{0:T(1024)}, f32[884736]{0:T(1024)}), (f32[552960]{0:T(1024)}, f32[331776]{0:T(1024)}, f32[1769472]{0:T(1024)}, f32[884736]{0:T(1024)})) %all-reduce.9.cloned.1.call-update) | async-done | bytes 14155792
  (188 shorter events, 72.1 us)
Async XLA Ops:
  7.2 63.9 %all-gather.10.cloned.1.call-start = ((), (), s32[]{:S(2)}) async-start(), calls=%async_computation.4 | async-start | bytes 2280960 | tf_op jit(solution)/shard_map/all_gather | solution.py:41
  8.7 202.8 %all-gather.8.cloned.1.call-start = ((), (), s32[]{:S(2)}) async-start(), calls=%async_computation.2 | async-start | bytes 1824768 | tf_op jit(solution)/shard_map/all_gather | solution.py:44
  9.4 206.8 %all-gather.6.cloned.1.call-start = ((), (), s32[]{:S(2)}) async-start(), calls=%async_computation.1 | async-start | bytes 3649536 | tf_op jit(solution)/shard_map/all_gather | solution.py:43
  10.2 649.3 %reduce-scatter.2.cloned.1.call-start = ((), (), s32[]{:S(2)}) async-start(), calls=%async_computation.3 | async-start | bytes 7864320 | tf_op jit(solution)/shard_map/reduce_scatter | solution.py:182
  53.8 5.3 copy-start.34
  59.9 149.4 %copy-start.27 = (f32[256,64]{0,1:T(8,128)}, f32[256,64]{0,1:T(8,128)S(1)}, u32[]{:S(2)}) copy-start(f32[256,64]{0,1:T(8,128)S(1)} %get-tuple-element.52) | copy-start | bytes 196612
  85.6 3.1 copy-start.8
  86.0 2.9 copy-start.29
  88.9 21.3 %copy-start.39 = (bf16[10368]{0:T(1024)(128)(2,1)S(1)}, bf16[10368]{0:T(1024)(128)(2,1)}, u32[]{:S(2)}) copy-start(bf16[10368]{0:T(1024)(128)(2,1)} %param.9) | copy-start | bytes 62212
  88.9 21.3 %copy-start.4 = (bf16[8,256,576]{1,2,0:T(8,128)(2,1)S(1)}, bf16[8,256,576]{1,2,0:T(8,128)(2,1)}, u32[]{:S(2)}) copy-start(bf16[8,256,576]{1,2,0:T(8,128)(2,1)} %param.7) | copy-start | bytes 7077892
  89.3 23.6 %copy-start.12 = (bf16[8,256,192]{1,0,2:T(8,128)(2,1)}, bf16[8,256,192]{1,0,2:T(8,128)(2,1)S(1)}, u32[]{:S(2)}) copy-start(bf16[8,256,192]{1,0,2:T(8,128)(2,1)S(1)} %fusion.31) | copy-start | bytes 2359300
  89.5 20.7 %collective-permute-start = (bf16[8,256,384]{1,0,2:T(8,128)(2,1)S(1)}, bf16[8,256,384]{1,0,2:T(8,128)(2,1)S(1)}, u32[]{:S(2)}, u32[]{:S(2)}) collective-permute-start(bf16[8,256,384]{1,0,2:T(8,128)(2,1)S(1)} %pad_maximum_fusion.11), channel_id=1, source_target_pairs={{0,1},{1,2},{2,3},{3,0},{4,5},{5,6},{6,7},{7,4},{8,9},{9,10},{10,1... | collective-permute-start | bytes 4718600 | tf_op jit(solution)/shard_map/ppermute | solution.py:100
  110.2 23.1 %copy-start.18 = (bf16[8,256,384]{1,0,2:T(8,128)(2,1)}, bf16[8,256,384]{1,0,2:T(8,128)(2,1)S(1)}, u32[]{:S(2)}) copy-start(bf16[8,256,384]{1,0,2:T(8,128)(2,1)S(1)} %collective-permute-done) | copy-start | bytes 4718596
  110.2 23.1 %collective-permute-start.1 = (bf16[8,256,384]{1,0,2:T(8,128)(2,1)S(1)}, bf16[8,256,384]{1,0,2:T(8,128)(2,1)}, u32[]{:S(2)}, u32[]{:S(2)}) collective-permute-start(bf16[8,256,384]{1,0,2:T(8,128)(2,1)S(1)} %collective-permute-done), channel_id=1, source_target_pairs={{0,1},{1,2},{2,3},{3,0},{4,5},{5,6},{6,7},{7,4},{8,9},{9,10},{10,1... | collective-permute-start | bytes 4718600 | tf_op jit(solution)/shard_map/ppermute | solution.py:100
  133.3 89.9 %collective-permute-start.2 = (bf16[8,256,384]{1,0,2:T(8,128)(2,1)}, bf16[8,256,384]{1,0,2:T(8,128)(2,1)}, u32[]{:S(2)}, u32[]{:S(2)}) collective-permute-start(bf16[8,256,384]{1,0,2:T(8,128)(2,1)} %collective-permute-done.1), channel_id=1, source_target_pairs={{0,1},{1,2},{2,3},{3,0},{4,5},{5,6},{6,7},{7,4},{8,9},{9,10},{10,1... | collective-permute-start | bytes 4718600 | tf_op jit(solution)/shard_map/ppermute | solution.py:100
  194.3 3.5 copy-start.7
  202.9 2.3 slice-start.4
  211.5 25.5 %copy-start.5 = (bf16[8,256,3,3,64]{1,4,3,2,0:T(8,128)(2,1)}, bf16[8,256,3,3,64]{1,4,3,2,0:T(8,128)(2,1)S(1)}, u32[]{:S(2)}) copy-start(bf16[8,256,3,3,64]{1,4,3,2,0:T(8,128)(2,1)S(1)} %fusion.18) | copy-start | bytes 7077892
  223.1 3.4 copy-start.19
  223.1 3.7 copy-start.13
  233.4 30.7 %copy-start.2 = (bf16[8,1024,192]{1,2,0:T(8,128)(2,1)}, bf16[8,1024,192]{1,2,0:T(8,128)(2,1)S(1)}, u32[]{:S(2)}) copy-start(bf16[8,1024,192]{1,2,0:T(8,128)(2,1)S(1)} %copy.60) | copy-start | bytes 9437188
  264.1 26.4 %copy-start.14 = (bf16[8,1024,192]{1,2,0:T(8,128)(2,1)S(1)}, bf16[8,1024,192]{1,2,0:T(8,128)(2,1)}, u32[]{:S(2)}) copy-start(bf16[8,1024,192]{1,2,0:T(8,128)(2,1)} %copy.59) | copy-start | bytes 9437188
  320.3 4.0 copy-start.21
  324.3 5.5 copy-start.10
  324.3 5.6 copy-start.20
  324.3 5.6 copy-start.40
  329.9 14.0 %copy-start = (f32[2048,576]{0,1:T(8,128)}, f32[2048,576]{0,1:T(8,128)S(1)}, u32[]{:S(2)}) copy-start(f32[2048,576]{0,1:T(8,128)S(1)} %get-tuple-element.60) | copy-start | bytes 14155780
  329.9 49.0 %copy-start.36 = (f32[2048]{0:T(1024)}, f32[2048]{0:T(1024)S(1)}, u32[]{:S(2)}) copy-start(f32[2048]{0:T(1024)S(1)} %add_rsqrt_fusion) | copy-start | bytes 24580
  365.4 13.5 %copy-start.1 = (f32[2048,576]{0,1:T(8,128)S(1)}, f32[2048,576]{0,1:T(8,128)}, u32[]{:S(2)}) copy-start(f32[2048,576]{0,1:T(8,128)} %copy-done) | copy-start | bytes 14155780
  365.4 13.5 %copy-start.15 = (bf16[8,72,8,256]{3,2,0,1:T(8,128)(2,1)S(1)}, bf16[8,72,8,256]{3,2,0,1:T(8,128)(2,1)}, u32[]{:S(2)}) copy-start(bf16[8,72,8,256]{3,2,0,1:T(8,128)(2,1)} %copy.96) | copy-start | bytes 7077892
  473.5 6.2 copy-start.33
  479.7 59.9 %copy-start.6 = (f32[1024,64]{0,1:T(8,128)S(1)}, f32[1024,64]{0,1:T(8,128)}, u32[]{:S(2)}) copy-start(f32[1024,64]{0,1:T(8,128)} %get-tuple-element.50) | copy-start | bytes 786436
  559.1 2.4 copy-start.26
  579.5 338.4 %all-reduce.9.cloned.1.call-start = ((), (), s32[]{:S(2)}) async-start(), calls=%async_computation.5 | async-start | bytes 28311552
  580.8 5.1 copy-start.16
  594.9 5.4 copy-start.37
  594.9 5.4 copy-start.41
  612.4 4.5 copy-start.11
  616.8 8.6 copy-start.3
  625.4 18.2 %copy-start.28 = (f32[256,64]{0,1:T(8,128)S(1)}, f32[256,64]{0,1:T(8,128)}, u32[]{:S(2)}) copy-start(f32[256,64]{0,1:T(8,128)} %copy-done.27) | copy-start | bytes 196612
  649.1 2.6 slice-start.2
  649.4 2.3 slice-start.3
  651.7 5.0 slice-start.5
  656.8 5.5 copy-start.35
  670.8 12.3 %slice-start = ((s8[4718592]{0:T(1024)(128)(4,1)}), s8[524288]{0:T(1024)(128)(4,1)S(1)}, s32[]{:S(2)}) async-start(s8[4718592]{0:T(1024)(128)(4,1)} %bitcast.168), calls=%async_computation.6 | async-start | bytes 1048576
  672.4 10.8 %slice-start.1 = ((s8[4718592]{0:T(1024)(128)(4,1)}), s8[4194304]{0:T(1024)(128)(4,1)S(1)}, s32[]{:S(2)}) async-start(s8[4718592]{0:T(1024)(128)(4,1)} %bitcast.168), calls=%async_computation.7 | async-start | bytes 8388608
  681.6 2.5 copy-start.23
  681.6 3.0 copy-start.25
  (10 other events, 15.9 us)
Sparse Core Ops, SparseCore 0:
  11.4 59.5 all-gather.9
  73.9 55.3 all-gather.7
  132.2 61.0 all-gather.5
  579.7 54.6 reduce-scatter.1
  671.0 246.9 all-reduce.8
